TPU v7x, 128 devices: a whole 4x4x4 slice. The times are simulated.
128 devices in a mesh: wide: 8 (over x, core), rep: 16 (over y, z).
Axes of the slice: x: 4, y: 4, z: 4, core: 2. Of those that a mesh axis runs over, the one named last changes fastest.
Arguments:
- stretch_qkv: bfloat16 [16, 1536, 3, 5120], P('rep', 'wide'), may hold values from -60 to 60
- norm_gains: float32 [2, 5120], replicated, may hold values from 0.25 to 1.75
- cache: bfloat16 [256, 2, 192, 5120], P('rep', None, 'wide'), may hold values from -6 to 6
- cached_stretches: int32 [16], replicated, may hold values from 1 to 2, as said below
- block_slot: int32 [16, 16], replicated, may hold values from 0 to 255, as said below
- video_of_group: int32 [16], replicated, may hold values from 0 to 15, each once
Outputs:
- attended: bfloat16 [16, 1536, 5120], P('rep', 'wide')
Inputs may be any that keep to these rules, and one draw needn't show every extreme that they name: `cached_stretches`: each value is 1 to 2; some video has exactly 2. Block b of video u holds that video's cached tokens b * 192 to (b + 1) * 192 - 1, oldest first; it is cache row block_slot[u, b], owned by group block_slot[u, b] // 16. Every group owns exactly 1 block of every video; no two blocks share a row.
All inputs are finite; a program needn't handle non-finite values.
Results may differ from a plain program's by a relative error of at most 0.011.
Values may be sent and summed in bfloat16 or wider, within the bound.
A program may use at most 128 MiB of HBM per device.

v0:
```python
import math
import jax
import jax.numpy as jnp
from jax import lax
from jax.sharding import PartitionSpec as P

HD = 128
epsilon = 1e-06


def normalize(stretch_rows, gains_row):
    widened = stretch_rows.astype(jnp.float32)
    mean_square = jnp.mean(widened * widened, axis=-1, keepdims=True)
    return (widened * lax.rsqrt(mean_square + epsilon) * gains_row).astype(jnp.bfloat16)


def attend_block(query_rows, all_keys, all_values, usable):
    scores = jnp.einsum(
        "qhd,khd->hqk", query_rows, all_keys, preferred_element_type=jnp.float32
    ) * HD ** (-0.5)
    scores = jnp.where(usable[None, None, :], scores, -jnp.inf)
    row_max = jnp.max(scores, axis=-1, keepdims=True)
    weights = jnp.exp(scores - row_max)
    row_total = jnp.sum(weights, axis=-1, keepdims=True)
    mixed = jnp.einsum(
        "hqk,khd->qhd", weights.astype(jnp.bfloat16), all_values, preferred_element_type=jnp.float32
    )
    return (mixed / jnp.transpose(row_total, (1, 0, 2))).astype(jnp.bfloat16)


def body(stretch_qkv, norm_gains, cache, cached_stretches, block_slot, video_of_group):
    rep_count = lax.axis_size("rep")
    wide_count = lax.axis_size("wide")
    own_group = lax.axis_index("rep")
    stretch_rows = stretch_qkv[0]
    width = stretch_rows.shape[-1]
    head_width = width // wide_count
    heads_dev = head_width // HD
    queries = normalize(stretch_rows[:, 0], norm_gains[0])
    keys_new = normalize(stretch_rows[:, 1], norm_gains[1])
    framed = jnp.stack([queries, keys_new, stretch_rows[:, 2]], axis=1)
    headed = lax.all_to_all(framed, "wide", split_axis=2, concat_axis=0, tiled=True)
    stretch_len = headed.shape[0]
    slots_dev = cache.shape[0]
    cap_dev = slots_dev // rep_count
    blocks = block_slot.shape[1]
    block_wide = cache.shape[2]
    block_len = block_wide * wide_count
    group_ids = jnp.arange(rep_count, dtype=jnp.int32)
    pick_video = (video_of_group[:, None] == group_ids[None, :]).astype(jnp.int32)
    slot_table = jnp.dot(pick_video, block_slot)
    owned_here = (slot_table // slots_dev == own_group).astype(jnp.int32)
    rank_in_owner = jnp.cumsum(owned_here, axis=1) - owned_here
    local_slot = slot_table % slots_dev
    chosen = jnp.stack([jnp.sum(owned_here * (rank_in_owner == 0) * local_slot, axis=1)], axis=1)
    outgoing = cache[chosen.reshape(-1)].reshape((rep_count, cap_dev) + cache.shape[1:])
    split_heads = outgoing.reshape(rep_count, cap_dev, 2, block_wide, wide_count, head_width)
    moved = jnp.moveaxis(split_heads, 4, 0).reshape(
        wide_count * rep_count, cap_dev, 2, block_wide, head_width
    )
    received = lax.all_to_all(moved, ("wide", "rep"), split_axis=0, concat_axis=0, tiled=True)
    received = received.reshape(wide_count, rep_count, cap_dev, 2, block_wide, head_width)
    arrived = jnp.transpose(received, (1, 2, 3, 0, 4, 5)).reshape(
        rep_count, cap_dev, 2, block_len, head_width
    )
    is_me = (group_ids == own_group).astype(jnp.int32)
    own_table = jnp.sum(slot_table * is_me[:, None], axis=0)
    own_video = jnp.sum(video_of_group * is_me)
    own_count = jnp.sum(cached_stretches * (group_ids == own_video).astype(jnp.int32))
    owners = own_table // slots_dev
    block_order = jnp.arange(blocks, dtype=jnp.int32)
    before = jnp.sum(
        (
            (owners[:, None] == owners[None, :]) & (block_order[:, None] > block_order[None, :])
        ).astype(jnp.int32),
        axis=1,
    )
    flat_index = owners * cap_dev + before
    history = arrived.reshape((rep_count * cap_dev,) + arrived.shape[2:])[flat_index]
    hist_span = blocks * block_len
    hist_keys = history[:, 0].reshape(hist_span, heads_dev, HD)
    hist_values = history[:, 1].reshape(hist_span, heads_dev, HD)
    new_queries = headed[:, 0].reshape(stretch_len, heads_dev, HD)
    new_keys = headed[:, 1].reshape(stretch_len, heads_dev, HD)
    new_values = headed[:, 2].reshape(stretch_len, heads_dev, HD)
    query_block = math.gcd(stretch_len, 256)
    blocks_q = new_queries.reshape(stretch_len // query_block, query_block, heads_dev, HD)
    all_keys = jnp.concatenate([hist_keys, new_keys], axis=0)
    all_values = jnp.concatenate([hist_values, new_values], axis=0)
    key_position = jnp.arange(hist_span + stretch_len, dtype=jnp.int32)
    usable = (key_position < own_count * stretch_len) | (key_position >= hist_span)
    attended = lax.map(lambda piece: attend_block(piece, all_keys, all_values, usable), blocks_q)
    attended = attended.reshape(stretch_len, head_width)
    returned = lax.all_to_all(attended, "wide", split_axis=0, concat_axis=1, tiled=True)
    return returned[None]


def solution(mesh):
    in_specs = (P("rep", "wide", None, None), P(), P("rep", None, "wide", None), P(), P(), P())
    out_specs = P("rep", "wide", None)
    return jax.shard_map(body, mesh=mesh, in_specs=in_specs, out_specs=out_specs, check_vma=False)
```

profile of v0, /device:TPU:8, one launch (start us, length us, event | category | flops | bytes accessed | tf_op | source)
XLA Modules:
  0.0 599.3 jit_solution(7813864269104856117)
XLA Ops:
  9.2 15.6 %copy.77 = bf16[192,3,5120]{0,1,2:T(4,128)(2,1)} copy(bf16[192,3,5120]{2,0,1:T(8,128)(2,1)} %pad_maximum_fusion) | data formatting | bytes 11796480 | tf_op jit(solution)/shard_map/stack | solution.py:41
  47.8 99.4 %all-to-all-done = bf16[192,3,5120]{0,1,2:T(4,128)(2,1)} async-done(((bf16[192,3,5120]{0,1,2:T(4,128)(2,1)}), bf16[192,3,5120]{0,1,2:T(4,128)(2,1)}, u32[]{:S(2)}, u32[]{:S(2)}) %all-to-all-start) | async-done | bytes 5898272 | tf_op jit(solution)/shard_map/all_to_all | solution.py:42
  159.1 15.7 %copy.94 = bf16[192,3,8,640]{3,0,2,1:T(8,128)(2,1)} copy(bf16[192,3,8,640]{0,1,3,2:T(4,128)(2,1)} %bitcast.3) | data formatting | bytes 11796480 | tf_op jit(solution)/shard_map/all_to_all | solution.py:42
  192.4 66.4 %all-to-all-done.1 = bf16[128,1,2,24,640]{4,3,2,1,0:T(8,128)(2,1)} async-done(((bf16[128,1,2,24,640]{4,3,2,1,0:T(8,128)(2,1)}), bf16[128,1,2,24,640]{4,3,2,1,0:T(8,128)(2,1)}, u32[]{:S(2)}, u32[]{:S(2)}) %all-to-all-start.1) | async-done | bytes 7864352 | tf_op jit(solution)/shard_map/all_to_all | solution.py:61
  344.9 214.1 %while.11 = (s32[]{:T(128)}, bf16[6,256,5,128]{3,1,2,0:T(8,128)(2,1)S(1)}, bf16[6,256,5,128]{3,1,2,0:T(8,128)(2,1)}, bf16[4608,5,128]{2,0,1:T(8,128)(2,1)}, bf16...) while((s32[]{:T(128)}, bf16[6,256,5,128]{3,1,2,0:T(8,128)(2,1)S(1)}, ...), condition=%wide.region_11.12_spmd.clone, body=%wide.region_8.11_spmd.clone.sunk | while | flops 3085118464 | bytes 106874992 | solution.py:92
  344.9 13.8 %fusion.66 = (f32[5,256]{1,0:T(8,128)S(1)}, f32[5,256,4608]{2,1,0:T(8,128)}) fusion(pred[4608]{0:T(1024)(128)(4,1)S(1)} %fusion.65, bf16[4608,5,128]{2,0,1:T(8,128)(2,1)} %get-tuple-element.178, bf16[6,256,5,128]{3,1,2,0:T(8,128)(2,1)} %get-tuple-element.177, s32[]{:T(128)} %get-tuple-element.168), kind=kOutput, calls=%fused_computation.5.clone.1 | convolution fusion | flops 1527642880 | bytes 29829120 | tf_op jit(solution)/shard_map/while/body/eval_jaxpr/qhd,khd->hqk/dot_general | solution.py:18
  358.7 10.9 %fusion.67 = f32[5,256]{1,0:T(8,128)S(1)} fusion(f32[5,256,4608]{2,1,0:T(8,128)} %get-tuple-element.159, f32[5,256]{1,0:T(8,128)S(1)} %get-tuple-element.160, pred[4608]{0:T(1024)(128)(4,1)S(1)} %fusion.65), kind=kLoop, calls=%fused_computation.6.clone.1 | loop fusion | flops 23591680 | bytes 23607808 | tf_op jit(solution)/shard_map/while/body/eval_jaxpr/reduce_sum | solution.py:24
  369.7 10.9 %fusion.68 = bf16[6,256,5,128]{3,1,2,0:T(8,128)(2,1)S(1)} fusion(bf16[6,256,5,128]{3,1,2,0:T(8,128)(2,1)S(1)} %get-tuple-element.169, s32[]{:T(128)} %get-tuple-element.168, bf16[4608,5,128]{2,0,1:T(8,128)(2,1)S(1)} %copy-done.5, f32[5,256,4608]{2,1,0:T(8,128)} %get-tuple-element.159, f32[5,256]{1,0:T(8,128)S(1)} %get-tuple-element.160, ...), kind=kOutput, calls=%fused_computation.14.clone.1 | convolution fusion | flops 1533870080 | bytes 29840388 | tf_op jit(solution)/shard_map/while/body/eval_jaxpr/hqk,khd->qhd/dot_general | solution.py:25
  380.6 13.8 %fusion.66 = (f32[5,256]{1,0:T(8,128)S(1)}, f32[5,256,4608]{2,1,0:T(8,128)}) fusion(pred[4608]{0:T(1024)(128)(4,1)S(1)} %fusion.65, bf16[4608,5,128]{2,0,1:T(8,128)(2,1)} %get-tuple-element.178, bf16[6,256,5,128]{3,1,2,0:T(8,128)(2,1)} %get-tuple-element.177, s32[]{:T(128)} %get-tuple-element.168), kind=kOutput, calls=%fused_computation.5.clone.1 | convolution fusion | flops 1527642880 | bytes 29829120 | tf_op jit(solution)/shard_map/while/body/eval_jaxpr/qhd,khd->hqk/dot_general | solution.py:18
  394.4 10.9 %fusion.67 = f32[5,256]{1,0:T(8,128)S(1)} fusion(f32[5,256,4608]{2,1,0:T(8,128)} %get-tuple-element.159, f32[5,256]{1,0:T(8,128)S(1)} %get-tuple-element.160, pred[4608]{0:T(1024)(128)(4,1)S(1)} %fusion.65), kind=kLoop, calls=%fused_computation.6.clone.1 | loop fusion | flops 23591680 | bytes 23607808 | tf_op jit(solution)/shard_map/while/body/eval_jaxpr/reduce_sum | solution.py:24
  405.4 10.9 %fusion.68 = bf16[6,256,5,128]{3,1,2,0:T(8,128)(2,1)S(1)} fusion(bf16[6,256,5,128]{3,1,2,0:T(8,128)(2,1)S(1)} %get-tuple-element.169, s32[]{:T(128)} %get-tuple-element.168, bf16[4608,5,128]{2,0,1:T(8,128)(2,1)S(1)} %copy-done.5, f32[5,256,4608]{2,1,0:T(8,128)} %get-tuple-element.159, f32[5,256]{1,0:T(8,128)S(1)} %get-tuple-element.160, ...), kind=kOutput, calls=%fused_computation.14.clone.1 | convolution fusion | flops 1533870080 | bytes 29840388 | tf_op jit(solution)/shard_map/while/body/eval_jaxpr/hqk,khd->qhd/dot_general | solution.py:25
  416.3 13.8 %fusion.66 = (f32[5,256]{1,0:T(8,128)S(1)}, f32[5,256,4608]{2,1,0:T(8,128)}) fusion(pred[4608]{0:T(1024)(128)(4,1)S(1)} %fusion.65, bf16[4608,5,128]{2,0,1:T(8,128)(2,1)} %get-tuple-element.178, bf16[6,256,5,128]{3,1,2,0:T(8,128)(2,1)} %get-tuple-element.177, s32[]{:T(128)} %get-tuple-element.168), kind=kOutput, calls=%fused_computation.5.clone.1 | convolution fusion | flops 1527642880 | bytes 29829120 | tf_op jit(solution)/shard_map/while/body/eval_jaxpr/qhd,khd->hqk/dot_general | solution.py:18
  430.1 10.9 %fusion.67 = f32[5,256]{1,0:T(8,128)S(1)} fusion(f32[5,256,4608]{2,1,0:T(8,128)} %get-tuple-element.159, f32[5,256]{1,0:T(8,128)S(1)} %get-tuple-element.160, pred[4608]{0:T(1024)(128)(4,1)S(1)} %fusion.65), kind=kLoop, calls=%fused_computation.6.clone.1 | loop fusion | flops 23591680 | bytes 23607808 | tf_op jit(solution)/shard_map/while/body/eval_jaxpr/reduce_sum | solution.py:24
  441.1 10.9 %fusion.68 = bf16[6,256,5,128]{3,1,2,0:T(8,128)(2,1)S(1)} fusion(bf16[6,256,5,128]{3,1,2,0:T(8,128)(2,1)S(1)} %get-tuple-element.169, s32[]{:T(128)} %get-tuple-element.168, bf16[4608,5,128]{2,0,1:T(8,128)(2,1)S(1)} %copy-done.5, f32[5,256,4608]{2,1,0:T(8,128)} %get-tuple-element.159, f32[5,256]{1,0:T(8,128)S(1)} %get-tuple-element.160, ...), kind=kOutput, calls=%fused_computation.14.clone.1 | convolution fusion | flops 1533870080 | bytes 29840388 | tf_op jit(solution)/shard_map/while/body/eval_jaxpr/hqk,khd->qhd/dot_general | solution.py:25
  452.0 13.8 %fusion.66 = (f32[5,256]{1,0:T(8,128)S(1)}, f32[5,256,4608]{2,1,0:T(8,128)}) fusion(pred[4608]{0:T(1024)(128)(4,1)S(1)} %fusion.65, bf16[4608,5,128]{2,0,1:T(8,128)(2,1)} %get-tuple-element.178, bf16[6,256,5,128]{3,1,2,0:T(8,128)(2,1)} %get-tuple-element.177, s32[]{:T(128)} %get-tuple-element.168), kind=kOutput, calls=%fused_computation.5.clone.1 | convolution fusion | flops 1527642880 | bytes 29829120 | tf_op jit(solution)/shard_map/while/body/eval_jaxpr/qhd,khd->hqk/dot_general | solution.py:18
  465.8 10.9 %fusion.67 = f32[5,256]{1,0:T(8,128)S(1)} fusion(f32[5,256,4608]{2,1,0:T(8,128)} %get-tuple-element.159, f32[5,256]{1,0:T(8,128)S(1)} %get-tuple-element.160, pred[4608]{0:T(1024)(128)(4,1)S(1)} %fusion.65), kind=kLoop, calls=%fused_computation.6.clone.1 | loop fusion | flops 23591680 | bytes 23607808 | tf_op jit(solution)/shard_map/while/body/eval_jaxpr/reduce_sum | solution.py:24
  476.8 10.9 %fusion.68 = bf16[6,256,5,128]{3,1,2,0:T(8,128)(2,1)S(1)} fusion(bf16[6,256,5,128]{3,1,2,0:T(8,128)(2,1)S(1)} %get-tuple-element.169, s32[]{:T(128)} %get-tuple-element.168, bf16[4608,5,128]{2,0,1:T(8,128)(2,1)S(1)} %copy-done.5, f32[5,256,4608]{2,1,0:T(8,128)} %get-tuple-element.159, f32[5,256]{1,0:T(8,128)S(1)} %get-tuple-element.160, ...), kind=kOutput, calls=%fused_computation.14.clone.1 | convolution fusion | flops 1533870080 | bytes 29840388 | tf_op jit(solution)/shard_map/while/body/eval_jaxpr/hqk,khd->qhd/dot_general | solution.py:25
  487.6 13.8 %fusion.66 = (f32[5,256]{1,0:T(8,128)S(1)}, f32[5,256,4608]{2,1,0:T(8,128)}) fusion(pred[4608]{0:T(1024)(128)(4,1)S(1)} %fusion.65, bf16[4608,5,128]{2,0,1:T(8,128)(2,1)} %get-tuple-element.178, bf16[6,256,5,128]{3,1,2,0:T(8,128)(2,1)} %get-tuple-element.177, s32[]{:T(128)} %get-tuple-element.168), kind=kOutput, calls=%fused_computation.5.clone.1 | convolution fusion | flops 1527642880 | bytes 29829120 | tf_op jit(solution)/shard_map/while/body/eval_jaxpr/qhd,khd->hqk/dot_general | solution.py:18
  501.5 10.9 %fusion.67 = f32[5,256]{1,0:T(8,128)S(1)} fusion(f32[5,256,4608]{2,1,0:T(8,128)} %get-tuple-element.159, f32[5,256]{1,0:T(8,128)S(1)} %get-tuple-element.160, pred[4608]{0:T(1024)(128)(4,1)S(1)} %fusion.65), kind=kLoop, calls=%fused_computation.6.clone.1 | loop fusion | flops 23591680 | bytes 23607808 | tf_op jit(solution)/shard_map/while/body/eval_jaxpr/reduce_sum | solution.py:24
  512.4 10.9 %fusion.68 = bf16[6,256,5,128]{3,1,2,0:T(8,128)(2,1)S(1)} fusion(bf16[6,256,5,128]{3,1,2,0:T(8,128)(2,1)S(1)} %get-tuple-element.169, s32[]{:T(128)} %get-tuple-element.168, bf16[4608,5,128]{2,0,1:T(8,128)(2,1)S(1)} %copy-done.5, f32[5,256,4608]{2,1,0:T(8,128)} %get-tuple-element.159, f32[5,256]{1,0:T(8,128)S(1)} %get-tuple-element.160, ...), kind=kOutput, calls=%fused_computation.14.clone.1 | convolution fusion | flops 1533870080 | bytes 29840388 | tf_op jit(solution)/shard_map/while/body/eval_jaxpr/hqk,khd->qhd/dot_general | solution.py:25
  523.3 13.8 %fusion.66 = (f32[5,256]{1,0:T(8,128)S(1)}, f32[5,256,4608]{2,1,0:T(8,128)}) fusion(pred[4608]{0:T(1024)(128)(4,1)S(1)} %fusion.65, bf16[4608,5,128]{2,0,1:T(8,128)(2,1)} %get-tuple-element.178, bf16[6,256,5,128]{3,1,2,0:T(8,128)(2,1)} %get-tuple-element.177, s32[]{:T(128)} %get-tuple-element.168), kind=kOutput, calls=%fused_computation.5.clone.1 | convolution fusion | flops 1527642880 | bytes 29829120 | tf_op jit(solution)/shard_map/while/body/eval_jaxpr/qhd,khd->hqk/dot_general | solution.py:18
  537.2 10.9 %fusion.67 = f32[5,256]{1,0:T(8,128)S(1)} fusion(f32[5,256,4608]{2,1,0:T(8,128)} %get-tuple-element.159, f32[5,256]{1,0:T(8,128)S(1)} %get-tuple-element.160, pred[4608]{0:T(1024)(128)(4,1)S(1)} %fusion.65), kind=kLoop, calls=%fused_computation.6.clone.1 | loop fusion | flops 23591680 | bytes 23607808 | tf_op jit(solution)/shard_map/while/body/eval_jaxpr/reduce_sum | solution.py:24
  548.1 10.9 %fusion.68 = bf16[6,256,5,128]{3,1,2,0:T(8,128)(2,1)S(1)} fusion(bf16[6,256,5,128]{3,1,2,0:T(8,128)(2,1)S(1)} %get-tuple-element.169, s32[]{:T(128)} %get-tuple-element.168, bf16[4608,5,128]{2,0,1:T(8,128)(2,1)S(1)} %copy-done.5, f32[5,256,4608]{2,1,0:T(8,128)} %get-tuple-element.159, f32[5,256]{1,0:T(8,128)S(1)} %get-tuple-element.160, ...), kind=kOutput, calls=%fused_computation.14.clone.1 | convolution fusion | flops 1533870080 | bytes 29840388 | tf_op jit(solution)/shard_map/while/body/eval_jaxpr/hqk,khd->qhd/dot_general | solution.py:25
  566.6 29.3 %all_to_all.39 = bf16[8,192,640]{2,1,0:T(8,128)(2,1)S(1)} all-to-all(bf16[8,192,640]{2,1,0:T(8,128)(2,1)} %all_to_all.33), channel_id=1, replica_groups=mesh['wide'=8,'rep'=16] {'wide'}, dimensions={0} | all-to-all | bytes 3932160 | tf_op jit(solution)/shard_map/all_to_all | solution.py:94
  (82 shorter events, 158.0 us)
Async XLA Ops:
  0.0 30.1 %copy-start = (s32[16,16]{1,0:T(8,128)S(1)}, s32[16,16]{1,0:T(8,128)}, u32[]{:S(2)}) copy-start(s32[16,16]{1,0:T(8,128)} %param.12) | copy-start | bytes 3076
  0.0 4.9 copy-start.2
  0.0 4.8 copy-start.8
  24.8 5.3 copy-start.9
  24.8 122.3 %all-to-all-start = ((bf16[192,3,5120]{0,1,2:T(4,128)(2,1)}), bf16[192,3,5120]{0,1,2:T(4,128)(2,1)}, u32[]{:S(2)}, u32[]{:S(2)}) async-start(bf16[192,3,5120]{0,1,2:T(4,128)(2,1)} %copy.77), calls=%async_computation | async-start | bytes 20971520 | tf_op jit(solution)/shard_map/all_to_all | solution.py:42
  147.1 9.7 %copy-start.10 = (s32[16]{0:T(128)S(1)}, s32[16]{0:T(128)}, u32[]{:S(2)}) copy-start(s32[16]{0:T(128)} %param.11) | copy-start | bytes 196
  147.1 111.7 %all-to-all-start.1 = ((bf16[128,1,2,24,640]{4,3,2,1,0:T(8,128)(2,1)}), bf16[128,1,2,24,640]{4,3,2,1,0:T(8,128)(2,1)}, u32[]{:S(2)}, u32[]{:S(2)}) async-start(bf16[128,1,2,24,640]{4,3,2,1,0:T(8,128)(2,1)} %bitcast.97), calls=%async_computation.1 | async-start | bytes 15728640 | tf_op jit(solution)/shard_map/all_to_all | solution.py:61
  288.6 9.9 %copy-start.4 = (bf16[1536,1,640]{0,2,1:T(8,128)(2,1)S(1)}, bf16[1536,1,640]{0,2,1:T(8,128)(2,1)}, u32[]{:S(2)}) copy-start(bf16[1536,1,640]{0,2,1:T(8,128)(2,1)} %copy.85) | copy-start | bytes 5898244
  321.0 9.8 %copy-start.3 = (bf16[1536,1,640]{0,2,1:T(8,128)(2,1)S(1)}, bf16[1536,1,640]{0,2,1:T(8,128)(2,1)}, u32[]{:S(2)}) copy-start(bf16[1536,1,640]{0,2,1:T(8,128)(2,1)} %copy.87) | copy-start | bytes 5898244
  335.9 9.0 %copy-start.6 = (bf16[6,256,5,128]{3,1,2,0:T(8,128)(2,1)S(1)}, bf16[6,256,5,128]{3,1,2,0:T(8,128)(2,1)}, u32[]{:S(2)}) copy-start(bf16[6,256,5,128]{3,1,2,0:T(8,128)(2,1)} %custom-call.4) | copy-start | bytes 5898244
  358.7 10.9 %copy-start.5 = (bf16[4608,5,128]{2,0,1:T(8,128)(2,1)S(1)}, bf16[4608,5,128]{2,0,1:T(8,128)(2,1)}, u32[]{:S(2)}) copy-start(bf16[4608,5,128]{2,0,1:T(8,128)(2,1)} %get-tuple-element.179) | copy-start | bytes 17694724 | tf_op jit(solution)/shard_map/while
  394.4 10.9 %copy-start.5 = (bf16[4608,5,128]{2,0,1:T(8,128)(2,1)S(1)}, bf16[4608,5,128]{2,0,1:T(8,128)(2,1)}, u32[]{:S(2)}) copy-start(bf16[4608,5,128]{2,0,1:T(8,128)(2,1)} %get-tuple-element.179) | copy-start | bytes 17694724 | tf_op jit(solution)/shard_map/while
  430.1 10.9 %copy-start.5 = (bf16[4608,5,128]{2,0,1:T(8,128)(2,1)S(1)}, bf16[4608,5,128]{2,0,1:T(8,128)(2,1)}, u32[]{:S(2)}) copy-start(bf16[4608,5,128]{2,0,1:T(8,128)(2,1)} %get-tuple-element.179) | copy-start | bytes 17694724 | tf_op jit(solution)/shard_map/while
  465.8 10.9 %copy-start.5 = (bf16[4608,5,128]{2,0,1:T(8,128)(2,1)S(1)}, bf16[4608,5,128]{2,0,1:T(8,128)(2,1)}, u32[]{:S(2)}) copy-start(bf16[4608,5,128]{2,0,1:T(8,128)(2,1)} %get-tuple-element.179) | copy-start | bytes 17694724 | tf_op jit(solution)/shard_map/while
  501.5 10.9 %copy-start.5 = (bf16[4608,5,128]{2,0,1:T(8,128)(2,1)S(1)}, bf16[4608,5,128]{2,0,1:T(8,128)(2,1)}, u32[]{:S(2)}) copy-start(bf16[4608,5,128]{2,0,1:T(8,128)(2,1)} %get-tuple-element.179) | copy-start | bytes 17694724 | tf_op jit(solution)/shard_map/while
  537.2 10.9 %copy-start.5 = (bf16[4608,5,128]{2,0,1:T(8,128)(2,1)S(1)}, bf16[4608,5,128]{2,0,1:T(8,128)(2,1)}, u32[]{:S(2)}) copy-start(bf16[4608,5,128]{2,0,1:T(8,128)(2,1)} %get-tuple-element.179) | copy-start | bytes 17694724 | tf_op jit(solution)/shard_map/while
  559.0 1.3 copy-start.7
  563.2 36.1 %copy-start.1 = (s32[16,16]{1,0:T(8,128)S(1)}, s32[16,16]{1,0:T(8,128)}, u32[]{:S(2)}) copy-start(s32[16,16]{1,0:T(8,128)} %param.12) | copy-start | bytes 3076
where the time goes:
time: 602 us; the launch traced here: 599 us
  waiting for transfers between devices  166 us (28%)
  local copies, waits for them, and re-layouts  155 us (26%)
  matrix products  148 us (25%)
  other arithmetic  85.8 us (14%)
  blocking collectives  29.3 us (5%)
  starting transfers between devices  14.3 us (2%)
    all_to_all x1, waiting for transfers between devices, body(): lax.all_to_all(framed, 'wide', split_axis=2, concat_axis=0, tiled=True)  99.4 us
    dot_general x6, matrix products, attend_block(): jnp.einsum('qhd,khd->hqk', query_rows, all_keys, preferred_element_type=j...  83.1 us
    all_to_all x1, waiting for transfers between devices, body(): lax.all_to_all(moved, ('wide', 'rep'), split_axis=0, concat_axis=0, tiled...  66.4 us
    reduce_sum x6, other arithmetic, attend_block(): row_total = jnp.sum(weights, axis=-1, keepdims=True)  65.6 us
    dot_general x6, matrix products, attend_block(): jnp.einsum('hqk,khd->qhd', weights.astype(jnp.bfloat16), all_values, pref...  65.1 us
    all_to_all x1, blocking collectives, body(): lax.all_to_all(attended, 'wide', split_axis=0, concat_axis=1, tiled=True)  29.3 us
    unnamed x24, local copies, waits for them, and re-layouts  26 us
    all_to_all x1, local copies, waits for them, and re-layouts, body(): lax.all_to_all(framed, 'wide', split_axis=2, concat_axis=0, tiled=True)  15.7 us
  transfers between devices with their start and end apart: 2, of which 2 were waited for; matrix products, arithmetic and copies ran while one was open for 9% of the time, Pallas kernels for 0%

commit v1 on v0

--- a/solution.py
+++ b/solution.py
@@ -6,6 +6,9 @@
 
 HD = 128
 epsilon = 1e-06
+fit_the_groups = lambda mat: jnp.concatenate(
+    lax.all_to_all(jnp.stack(jnp.split(mat, lax.psum(1, "wide"), axis=2), 0), "wide", 0, 0), 0
+)
 
 
 def normalize(stretch_rows, gains_row):
@@ -39,7 +42,7 @@
     queries = normalize(stretch_rows[:, 0], norm_gains[0])
     keys_new = normalize(stretch_rows[:, 1], norm_gains[1])
     framed = jnp.stack([queries, keys_new, stretch_rows[:, 2]], axis=1)
-    headed = lax.all_to_all(framed, "wide", split_axis=2, concat_axis=0, tiled=True)
+    headed = fit_the_groups(framed)
     stretch_len = headed.shape[0]
     slots_dev = cache.shape[0]
     cap_dev = slots_dev // rep_count

time: 602 us -> 542 us (0.900)
  waiting for transfers between devices: 166 us -> 132 us
  local copies, waits for them, and re-layouts: 155 us -> 132 us
    all_to_all x1, waiting for transfers between devices: 99.4 us -> 50.1 us  [lax.all_to_all(jnp.stack(jnp.split(mat, lax.psum(1, 'wide'), axis=2), 0),...]
    all_to_all x1, waiting for transfers between devices: 66.4 us -> 81.8 us  [body(): lax.all_to_all(moved, ('wide', 'rep'), split_axis=0, concat_axis=0, tiled...]
    another operation x1, local copies, waits for them, and re-layouts: 15.6 us -> 0.95 us  [jnp.stack(jnp.split(mat, lax.psum(1, 'wide'), axis=2), 0)]
    all_to_all x1, local copies, waits for them, and re-layouts: 15.7 us -> 3.21 us  [lax.all_to_all(jnp.stack(jnp.split(mat, lax.psum(1, 'wide'), axis=2), 0),...]
    unnamed x24 -> x31, local copies, waits for them, and re-layouts: 26 us -> 32.7 us
  transfers between devices with their start and end apart: 2 -> 2, of which waited for: 2 -> 2; matrix products, arithmetic and copies ran while one was open for 9% -> 7% of each run, Pallas kernels for 0% -> 0%
where the time goes in v1:
time: 542 us; the launch traced here: 540 us
  matrix products  148 us (27%)
  local copies, waits for them, and re-layouts  132 us (24%)
  waiting for transfers between devices  132 us (24%)
  other arithmetic  83.6 us (15%)
  blocking collectives  29.3 us (5%)
  starting transfers between devices  13.9 us (3%)
    dot_general x6, matrix products, attend_block(): jnp.einsum('qhd,khd->hqk', query_rows, all_keys, preferred_element_type=j...  83.1 us
    all_to_all x1, waiting for transfers between devices, body(): lax.all_to_all(moved, ('wide', 'rep'), split_axis=0, concat_axis=0, tiled...  81.8 us
    reduce_sum x6, other arithmetic, attend_block(): row_total = jnp.sum(weights, axis=-1, keepdims=True)  65.6 us
    dot_general x6, matrix products, attend_block(): jnp.einsum('hqk,khd->qhd', weights.astype(jnp.bfloat16), all_values, pref...  65.1 us
    all_to_all x1, waiting for transfers between devices, lax.all_to_all(jnp.stack(jnp.split(mat, lax.psum(1, 'wide'), axis=2), 0),...  50.1 us
    unnamed x31, local copies, waits for them, and re-layouts  32.7 us
    all_to_all x1, blocking collectives, body(): lax.all_to_all(attended, 'wide', split_axis=0, concat_axis=1, tiled=True)  29.3 us
    slice x2, local copies, waits for them, and re-layouts, body(): hist_values = history[:, 1].reshape(hist_span, heads_dev, HD)  14.1 us
  transfers between devices with their start and end apart: 2, of which 2 were waited for; matrix products, arithmetic and copies ran while one was open for 7% of the time, Pallas kernels for 0%

profile of v1, /device:TPU:8, one launch (start us, length us, event | category | flops | bytes accessed | tf_op | source)
XLA Modules:
  0.0 539.6 jit_solution(7226932671893427366)
XLA Ops:
  37.4 50.1 %all-to-all-done = bf16[8,192,3,640]{3,1,2,0:T(8,128)(2,1)} async-done(((bf16[8,192,3,640]{3,1,2,0:T(8,128)(2,1)}), bf16[8,192,3,640]{3,1,2,0:T(8,128)(2,1)}, u32[]{:S(2)}, u32[]{:S(2)}) %all-to-all-start) | async-done | bytes 5898272 | tf_op jit(solution)/shard_map/all_to_all | solution.py:10
  117.3 81.8 %all-to-all-done.1 = bf16[128,1,2,24,640]{4,3,2,1,0:T(8,128)(2,1)} async-done(((bf16[128,1,2,24,640]{4,3,2,1,0:T(8,128)(2,1)}), bf16[128,1,2,24,640]{4,3,2,1,0:T(8,128)(2,1)}, u32[]{:S(2)}, u32[]{:S(2)}) %all-to-all-start.1) | async-done | bytes 7864352 | tf_op jit(solution)/shard_map/all_to_all | solution.py:64
  228.9 9.9 %reshape_squeeze.12 = bf16[3072,5,128]{0,2,1:T(8,128)(2,1)} reshape(bf16[16,1,192,640]{2,0,3,1:T(8,128)(2,1)} %copy.75) | data formatting | bytes 7864320 | tf_op jit(solution)/shard_map/reshape;squeeze | solution.py:84
  261.3 9.8 %reshape_squeeze.14 = bf16[3072,5,128]{0,2,1:T(8,128)(2,1)} reshape(bf16[16,1,192,640]{2,0,3,1:T(8,128)(2,1)} %copy.77) | data formatting | bytes 7864320 | tf_op jit(solution)/shard_map/reshape;squeeze | solution.py:85
  285.2 214.1 %while.11 = (s32[]{:T(128)}, bf16[6,256,5,128]{3,1,2,0:T(8,128)(2,1)S(1)}, bf16[6,256,5,128]{3,1,2,0:T(8,128)(2,1)}, bf16[4608,5,128]{2,0,1:T(8,128)(2,1)}, bf16...) while((s32[]{:T(128)}, bf16[6,256,5,128]{3,1,2,0:T(8,128)(2,1)S(1)}, ...), condition=%wide.region_11.12_spmd.clone, body=%wide.region_8.11_spmd.clone.sunk | while | flops 3085118464 | bytes 106874992 | solution.py:95
  285.2 13.8 %fusion.74 = (f32[5,256]{1,0:T(8,128)S(1)}, f32[5,256,4608]{2,1,0:T(8,128)}) fusion(pred[4608]{0:T(1024)(128)(4,1)S(1)} %fusion.73, bf16[4608,5,128]{2,0,1:T(8,128)(2,1)} %get-tuple-element.174, bf16[6,256,5,128]{3,1,2,0:T(8,128)(2,1)} %get-tuple-element.173, s32[]{:T(128)} %get-tuple-element.164), kind=kOutput, calls=%fused_computation.5.clone.1 | convolution fusion | flops 1527642880 | bytes 29829120 | tf_op jit(solution)/shard_map/while/body/eval_jaxpr/qhd,khd->hqk/dot_general | solution.py:21
  299.0 10.9 %fusion.75 = f32[5,256]{1,0:T(8,128)S(1)} fusion(f32[5,256,4608]{2,1,0:T(8,128)} %get-tuple-element.155, f32[5,256]{1,0:T(8,128)S(1)} %get-tuple-element.156, pred[4608]{0:T(1024)(128)(4,1)S(1)} %fusion.73), kind=kLoop, calls=%fused_computation.6.clone.1 | loop fusion | flops 23591680 | bytes 23607808 | tf_op jit(solution)/shard_map/while/body/eval_jaxpr/reduce_sum | solution.py:27
  310.0 10.9 %fusion.76 = bf16[6,256,5,128]{3,1,2,0:T(8,128)(2,1)S(1)} fusion(bf16[6,256,5,128]{3,1,2,0:T(8,128)(2,1)S(1)} %get-tuple-element.165, s32[]{:T(128)} %get-tuple-element.164, bf16[4608,5,128]{2,0,1:T(8,128)(2,1)S(1)} %copy-done.5, f32[5,256,4608]{2,1,0:T(8,128)} %get-tuple-element.155, f32[5,256]{1,0:T(8,128)S(1)} %get-tuple-element.156, ...), kind=kOutput, calls=%fused_computation.14.clone.1 | convolution fusion | flops 1533870080 | bytes 29840388 | tf_op jit(solution)/shard_map/while/body/eval_jaxpr/hqk,khd->qhd/dot_general | solution.py:28
  320.9 13.8 %fusion.74 = (f32[5,256]{1,0:T(8,128)S(1)}, f32[5,256,4608]{2,1,0:T(8,128)}) fusion(pred[4608]{0:T(1024)(128)(4,1)S(1)} %fusion.73, bf16[4608,5,128]{2,0,1:T(8,128)(2,1)} %get-tuple-element.174, bf16[6,256,5,128]{3,1,2,0:T(8,128)(2,1)} %get-tuple-element.173, s32[]{:T(128)} %get-tuple-element.164), kind=kOutput, calls=%fused_computation.5.clone.1 | convolution fusion | flops 1527642880 | bytes 29829120 | tf_op jit(solution)/shard_map/while/body/eval_jaxpr/qhd,khd->hqk/dot_general | solution.py:21
  334.7 10.9 %fusion.75 = f32[5,256]{1,0:T(8,128)S(1)} fusion(f32[5,256,4608]{2,1,0:T(8,128)} %get-tuple-element.155, f32[5,256]{1,0:T(8,128)S(1)} %get-tuple-element.156, pred[4608]{0:T(1024)(128)(4,1)S(1)} %fusion.73), kind=kLoop, calls=%fused_computation.6.clone.1 | loop fusion | flops 23591680 | bytes 23607808 | tf_op jit(solution)/shard_map/while/body/eval_jaxpr/reduce_sum | solution.py:27
  345.6 10.9 %fusion.76 = bf16[6,256,5,128]{3,1,2,0:T(8,128)(2,1)S(1)} fusion(bf16[6,256,5,128]{3,1,2,0:T(8,128)(2,1)S(1)} %get-tuple-element.165, s32[]{:T(128)} %get-tuple-element.164, bf16[4608,5,128]{2,0,1:T(8,128)(2,1)S(1)} %copy-done.5, f32[5,256,4608]{2,1,0:T(8,128)} %get-tuple-element.155, f32[5,256]{1,0:T(8,128)S(1)} %get-tuple-element.156, ...), kind=kOutput, calls=%fused_computation.14.clone.1 | convolution fusion | flops 1533870080 | bytes 29840388 | tf_op jit(solution)/shard_map/while/body/eval_jaxpr/hqk,khd->qhd/dot_general | solution.py:28
  356.5 13.8 %fusion.74 = (f32[5,256]{1,0:T(8,128)S(1)}, f32[5,256,4608]{2,1,0:T(8,128)}) fusion(pred[4608]{0:T(1024)(128)(4,1)S(1)} %fusion.73, bf16[4608,5,128]{2,0,1:T(8,128)(2,1)} %get-tuple-element.174, bf16[6,256,5,128]{3,1,2,0:T(8,128)(2,1)} %get-tuple-element.173, s32[]{:T(128)} %get-tuple-element.164), kind=kOutput, calls=%fused_computation.5.clone.1 | convolution fusion | flops 1527642880 | bytes 29829120 | tf_op jit(solution)/shard_map/while/body/eval_jaxpr/qhd,khd->hqk/dot_general | solution.py:21
  370.4 10.9 %fusion.75 = f32[5,256]{1,0:T(8,128)S(1)} fusion(f32[5,256,4608]{2,1,0:T(8,128)} %get-tuple-element.155, f32[5,256]{1,0:T(8,128)S(1)} %get-tuple-element.156, pred[4608]{0:T(1024)(128)(4,1)S(1)} %fusion.73), kind=kLoop, calls=%fused_computation.6.clone.1 | loop fusion | flops 23591680 | bytes 23607808 | tf_op jit(solution)/shard_map/while/body/eval_jaxpr/reduce_sum | solution.py:27
  381.3 10.9 %fusion.76 = bf16[6,256,5,128]{3,1,2,0:T(8,128)(2,1)S(1)} fusion(bf16[6,256,5,128]{3,1,2,0:T(8,128)(2,1)S(1)} %get-tuple-element.165, s32[]{:T(128)} %get-tuple-element.164, bf16[4608,5,128]{2,0,1:T(8,128)(2,1)S(1)} %copy-done.5, f32[5,256,4608]{2,1,0:T(8,128)} %get-tuple-element.155, f32[5,256]{1,0:T(8,128)S(1)} %get-tuple-element.156, ...), kind=kOutput, calls=%fused_computation.14.clone.1 | convolution fusion | flops 1533870080 | bytes 29840388 | tf_op jit(solution)/shard_map/while/body/eval_jaxpr/hqk,khd->qhd/dot_general | solution.py:28
  392.2 13.8 %fusion.74 = (f32[5,256]{1,0:T(8,128)S(1)}, f32[5,256,4608]{2,1,0:T(8,128)}) fusion(pred[4608]{0:T(1024)(128)(4,1)S(1)} %fusion.73, bf16[4608,5,128]{2,0,1:T(8,128)(2,1)} %get-tuple-element.174, bf16[6,256,5,128]{3,1,2,0:T(8,128)(2,1)} %get-tuple-element.173, s32[]{:T(128)} %get-tuple-element.164), kind=kOutput, calls=%fused_computation.5.clone.1 | convolution fusion | flops 1527642880 | bytes 29829120 | tf_op jit(solution)/shard_map/while/body/eval_jaxpr/qhd,khd->hqk/dot_general | solution.py:21
  406.1 10.9 %fusion.75 = f32[5,256]{1,0:T(8,128)S(1)} fusion(f32[5,256,4608]{2,1,0:T(8,128)} %get-tuple-element.155, f32[5,256]{1,0:T(8,128)S(1)} %get-tuple-element.156, pred[4608]{0:T(1024)(128)(4,1)S(1)} %fusion.73), kind=kLoop, calls=%fused_computation.6.clone.1 | loop fusion | flops 23591680 | bytes 23607808 | tf_op jit(solution)/shard_map/while/body/eval_jaxpr/reduce_sum | solution.py:27
  417.0 10.9 %fusion.76 = bf16[6,256,5,128]{3,1,2,0:T(8,128)(2,1)S(1)} fusion(bf16[6,256,5,128]{3,1,2,0:T(8,128)(2,1)S(1)} %get-tuple-element.165, s32[]{:T(128)} %get-tuple-element.164, bf16[4608,5,128]{2,0,1:T(8,128)(2,1)S(1)} %copy-done.5, f32[5,256,4608]{2,1,0:T(8,128)} %get-tuple-element.155, f32[5,256]{1,0:T(8,128)S(1)} %get-tuple-element.156, ...), kind=kOutput, calls=%fused_computation.14.clone.1 | convolution fusion | flops 1533870080 | bytes 29840388 | tf_op jit(solution)/shard_map/while/body/eval_jaxpr/hqk,khd->qhd/dot_general | solution.py:28
  427.9 13.8 %fusion.74 = (f32[5,256]{1,0:T(8,128)S(1)}, f32[5,256,4608]{2,1,0:T(8,128)}) fusion(pred[4608]{0:T(1024)(128)(4,1)S(1)} %fusion.73, bf16[4608,5,128]{2,0,1:T(8,128)(2,1)} %get-tuple-element.174, bf16[6,256,5,128]{3,1,2,0:T(8,128)(2,1)} %get-tuple-element.173, s32[]{:T(128)} %get-tuple-element.164), kind=kOutput, calls=%fused_computation.5.clone.1 | convolution fusion | flops 1527642880 | bytes 29829120 | tf_op jit(solution)/shard_map/while/body/eval_jaxpr/qhd,khd->hqk/dot_general | solution.py:21
  441.8 10.9 %fusion.75 = f32[5,256]{1,0:T(8,128)S(1)} fusion(f32[5,256,4608]{2,1,0:T(8,128)} %get-tuple-element.155, f32[5,256]{1,0:T(8,128)S(1)} %get-tuple-element.156, pred[4608]{0:T(1024)(128)(4,1)S(1)} %fusion.73), kind=kLoop, calls=%fused_computation.6.clone.1 | loop fusion | flops 23591680 | bytes 23607808 | tf_op jit(solution)/shard_map/while/body/eval_jaxpr/reduce_sum | solution.py:27
  452.7 10.9 %fusion.76 = bf16[6,256,5,128]{3,1,2,0:T(8,128)(2,1)S(1)} fusion(bf16[6,256,5,128]{3,1,2,0:T(8,128)(2,1)S(1)} %get-tuple-element.165, s32[]{:T(128)} %get-tuple-element.164, bf16[4608,5,128]{2,0,1:T(8,128)(2,1)S(1)} %copy-done.5, f32[5,256,4608]{2,1,0:T(8,128)} %get-tuple-element.155, f32[5,256]{1,0:T(8,128)S(1)} %get-tuple-element.156, ...), kind=kOutput, calls=%fused_computation.14.clone.1 | convolution fusion | flops 1533870080 | bytes 29840388 | tf_op jit(solution)/shard_map/while/body/eval_jaxpr/hqk,khd->qhd/dot_general | solution.py:28
  463.6 13.8 %fusion.74 = (f32[5,256]{1,0:T(8,128)S(1)}, f32[5,256,4608]{2,1,0:T(8,128)}) fusion(pred[4608]{0:T(1024)(128)(4,1)S(1)} %fusion.73, bf16[4608,5,128]{2,0,1:T(8,128)(2,1)} %get-tuple-element.174, bf16[6,256,5,128]{3,1,2,0:T(8,128)(2,1)} %get-tuple-element.173, s32[]{:T(128)} %get-tuple-element.164), kind=kOutput, calls=%fused_computation.5.clone.1 | convolution fusion | flops 1527642880 | bytes 29829120 | tf_op jit(solution)/shard_map/while/body/eval_jaxpr/qhd,khd->hqk/dot_general | solution.py:21
  477.5 10.9 %fusion.75 = f32[5,256]{1,0:T(8,128)S(1)} fusion(f32[5,256,4608]{2,1,0:T(8,128)} %get-tuple-element.155, f32[5,256]{1,0:T(8,128)S(1)} %get-tuple-element.156, pred[4608]{0:T(1024)(128)(4,1)S(1)} %fusion.73), kind=kLoop, calls=%fused_computation.6.clone.1 | loop fusion | flops 23591680 | bytes 23607808 | tf_op jit(solution)/shard_map/while/body/eval_jaxpr/reduce_sum | solution.py:27
  488.4 10.9 %fusion.76 = bf16[6,256,5,128]{3,1,2,0:T(8,128)(2,1)S(1)} fusion(bf16[6,256,5,128]{3,1,2,0:T(8,128)(2,1)S(1)} %get-tuple-element.165, s32[]{:T(128)} %get-tuple-element.164, bf16[4608,5,128]{2,0,1:T(8,128)(2,1)S(1)} %copy-done.5, f32[5,256,4608]{2,1,0:T(8,128)} %get-tuple-element.155, f32[5,256]{1,0:T(8,128)S(1)} %get-tuple-element.156, ...), kind=kOutput, calls=%fused_computation.14.clone.1 | convolution fusion | flops 1533870080 | bytes 29840388 | tf_op jit(solution)/shard_map/while/body/eval_jaxpr/hqk,khd->qhd/dot_general | solution.py:28
  506.9 29.3 %all_to_all.26 = bf16[8,192,640]{2,1,0:T(8,128)(2,1)S(1)} all-to-all(bf16[8,192,640]{2,1,0:T(8,128)(2,1)} %all_to_all.20), channel_id=1, replica_groups=mesh['wide'=8,'rep'=16] {'wide'}, dimensions={0} | all-to-all | bytes 3932160 | tf_op jit(solution)/shard_map/all_to_all | solution.py:97
  (88 shorter events, 143.8 us)
Async XLA Ops:
  0.0 19.5 %copy-start = (s32[16,16]{1,0:T(8,128)S(1)}, s32[16,16]{1,0:T(8,128)}, u32[]{:S(2)}) copy-start(s32[16,16]{1,0:T(8,128)} %param.12) | copy-start | bytes 3076
  0.0 4.9 copy-start.2
  0.0 4.8 copy-start.8
  14.6 4.9 copy-start.9
  14.6 72.8 %all-to-all-start = ((bf16[8,192,3,640]{3,1,2,0:T(8,128)(2,1)}), bf16[8,192,3,640]{3,1,2,0:T(8,128)(2,1)}, u32[]{:S(2)}, u32[]{:S(2)}) async-start(bf16[8,192,3,640]{3,1,2,0:T(8,128)(2,1)} %fusion.36), calls=%async_computation | async-start | bytes 11796480 | tf_op jit(solution)/shard_map/all_to_all | solution.py:10
  87.4 9.7 %copy-start.10 = (s32[16]{0:T(128)S(1)}, s32[16]{0:T(128)}, u32[]{:S(2)}) copy-start(s32[16]{0:T(128)} %param.11) | copy-start | bytes 196
  87.4 111.7 %all-to-all-start.1 = ((bf16[128,1,2,24,640]{4,3,2,1,0:T(8,128)(2,1)}), bf16[128,1,2,24,640]{4,3,2,1,0:T(8,128)(2,1)}, u32[]{:S(2)}, u32[]{:S(2)}) async-start(bf16[128,1,2,24,640]{4,3,2,1,0:T(8,128)(2,1)} %bitcast.125), calls=%async_computation.1 | async-start | bytes 15728640 | tf_op jit(solution)/shard_map/all_to_all | solution.py:64
  228.9 9.9 %copy-start.4 = (bf16[1536,1,640]{0,2,1:T(8,128)(2,1)S(1)}, bf16[1536,1,640]{0,2,1:T(8,128)(2,1)}, u32[]{:S(2)}) copy-start(bf16[1536,1,640]{0,2,1:T(8,128)(2,1)} %copy.76) | copy-start | bytes 5898244
  261.3 9.8 %copy-start.3 = (bf16[1536,1,640]{0,2,1:T(8,128)(2,1)S(1)}, bf16[1536,1,640]{0,2,1:T(8,128)(2,1)}, u32[]{:S(2)}) copy-start(bf16[1536,1,640]{0,2,1:T(8,128)(2,1)} %copy.78) | copy-start | bytes 5898244
  276.2 9.0 %copy-start.6 = (bf16[6,256,5,128]{3,1,2,0:T(8,128)(2,1)S(1)}, bf16[6,256,5,128]{3,1,2,0:T(8,128)(2,1)}, u32[]{:S(2)}) copy-start(bf16[6,256,5,128]{3,1,2,0:T(8,128)(2,1)} %custom-call.5) | copy-start | bytes 5898244
  299.0 10.9 %copy-start.5 = (bf16[4608,5,128]{2,0,1:T(8,128)(2,1)S(1)}, bf16[4608,5,128]{2,0,1:T(8,128)(2,1)}, u32[]{:S(2)}) copy-start(bf16[4608,5,128]{2,0,1:T(8,128)(2,1)} %get-tuple-element.175) | copy-start | bytes 17694724 | tf_op jit(solution)/shard_map/while
  334.7 10.9 %copy-start.5 = (bf16[4608,5,128]{2,0,1:T(8,128)(2,1)S(1)}, bf16[4608,5,128]{2,0,1:T(8,128)(2,1)}, u32[]{:S(2)}) copy-start(bf16[4608,5,128]{2,0,1:T(8,128)(2,1)} %get-tuple-element.175) | copy-start | bytes 17694724 | tf_op jit(solution)/shard_map/while
  370.4 10.9 %copy-start.5 = (bf16[4608,5,128]{2,0,1:T(8,128)(2,1)S(1)}, bf16[4608,5,128]{2,0,1:T(8,128)(2,1)}, u32[]{:S(2)}) copy-start(bf16[4608,5,128]{2,0,1:T(8,128)(2,1)} %get-tuple-element.175) | copy-start | bytes 17694724 | tf_op jit(solution)/shard_map/while
  406.1 10.9 %copy-start.5 = (bf16[4608,5,128]{2,0,1:T(8,128)(2,1)S(1)}, bf16[4608,5,128]{2,0,1:T(8,128)(2,1)}, u32[]{:S(2)}) copy-start(bf16[4608,5,128]{2,0,1:T(8,128)(2,1)} %get-tuple-element.175) | copy-start | bytes 17694724 | tf_op jit(solution)/shard_map/while
  441.8 10.9 %copy-start.5 = (bf16[4608,5,128]{2,0,1:T(8,128)(2,1)S(1)}, bf16[4608,5,128]{2,0,1:T(8,128)(2,1)}, u32[]{:S(2)}) copy-start(bf16[4608,5,128]{2,0,1:T(8,128)(2,1)} %get-tuple-element.175) | copy-start | bytes 17694724 | tf_op jit(solution)/shard_map/while
  477.5 10.9 %copy-start.5 = (bf16[4608,5,128]{2,0,1:T(8,128)(2,1)S(1)}, bf16[4608,5,128]{2,0,1:T(8,128)(2,1)}, u32[]{:S(2)}) copy-start(bf16[4608,5,128]{2,0,1:T(8,128)(2,1)} %get-tuple-element.175) | copy-start | bytes 17694724 | tf_op jit(solution)/shard_map/while
  499.3 1.3 copy-start.7
  503.5 36.1 %copy-start.1 = (s32[16,16]{1,0:T(8,128)S(1)}, s32[16,16]{1,0:T(8,128)}, u32[]{:S(2)}) copy-start(s32[16,16]{1,0:T(8,128)} %param.12) | copy-start | bytes 3076
